TPU v7x, 512 devices: a whole 4x4x16 slice. The times are simulated.
512 devices in a mesh: lat: 32 (over z, core), ch: 16 (over y, x).
Axes of the slice: x: 4, y: 4, z: 16, core: 2. Of those that a mesh axis runs over, the one named last changes fastest.
Arguments:
- fields: bfloat16 [2, 704, 32, 1440], P(None, 'lat', 'ch'), may hold values from -6 to 6
- table: bfloat16 [704, 704, 352], P('lat', 'ch'), may hold values from -1 to 1, as said below
Outputs:
- coefficients: float32 [704, 704, 128], P('lat', 'ch')
Inputs may be any that keep to these rules, and one draw needn't show every extreme that they name: table[m, l, k] is zero wherever l < m.
All inputs are finite; a program needn't handle non-finite values.
Results may differ from a plain program's by a relative error of at most 0.005.
Values may be sent and summed in bfloat16 or wider, within the bound.
A program may use at most 64 MiB of HBM per device.

v0:
```python
import math

import jax
import jax.numpy as jnp
from jax import lax
from jax.sharding import PartitionSpec as P

MODES = 704


def fourier_table(nlon, modes):
    cols = jnp.arange(nlon, dtype=jnp.int32)[:, None]
    orders = jnp.arange(modes, dtype=jnp.int32)[None, :]
    phase = (cols * orders % nlon).astype(jnp.float32) * (2.0 * math.pi / nlon)
    factor = 1.0 / math.sqrt(nlon)
    return jnp.concatenate([jnp.cos(phase) * factor, -jnp.sin(phase) * factor], axis=1).astype(
        jnp.bfloat16
    )


def parity_project(block, parts, order_start, degree_start):
    order_count, degree_count, hemisphere = block.shape
    padding = degree_count % 2
    first_rows = block[:, 0::2]
    second_rows = block[:, 1::2]
    orders = order_start + jnp.arange(order_count, dtype=jnp.int32)[:, None, None]
    aligned = (degree_start - orders) % 2 == 0
    sym_table = jnp.where(aligned, first_rows, second_rows)
    anti_table = jnp.where(aligned, second_rows, first_rows)
    sym_coeffs = jnp.einsum(
        "mlk,bkcrm->mlbcr", sym_table, parts[:, :hemisphere], preferred_element_type=jnp.float32
    )
    anti_coeffs = jnp.einsum(
        "mlk,bkcrm->mlbcr", anti_table, parts[:, hemisphere:], preferred_element_type=jnp.float32
    )
    chosen = aligned[:, :, :, None, None]
    first_out = jnp.where(chosen, sym_coeffs, anti_coeffs)
    second_out = jnp.where(chosen, anti_coeffs, sym_coeffs)
    joined = jnp.stack([first_out, second_out], axis=2)
    joined = joined.reshape((order_count, degree_count + padding) + sym_coeffs.shape[2:])
    return joined


def shards(fields, table):
    batch, rows, chans, nlon = fields.shape
    slab, lblock, half = table.shape
    fourier = fourier_table(nlon, MODES)
    spectrum = jnp.einsum("brcj,jn->brcn", fields, fourier, preferred_element_type=jnp.float32)
    spectrum = spectrum.astype(jnp.bfloat16).reshape(batch, rows, chans, 2, MODES)
    moved = lax.all_to_all(spectrum, "lat", split_axis=4, concat_axis=1, tiled=True)
    north = moved[:, :half].astype(jnp.float32)
    south = moved[:, half:][:, ::-1].astype(jnp.float32)
    parts = jnp.concatenate(
        [(north + south).astype(jnp.bfloat16), (north - south).astype(jnp.bfloat16)], axis=1
    )
    order_start = lax.axis_index("lat") * slab
    degree_start = lax.axis_index("ch") * lblock
    gathered = parity_project(
        table, lax.all_gather(parts, "ch", axis=2, tiled=True), order_start, degree_start
    )
    return gathered.reshape(slab, lblock, -1)


def solution(mesh):
    return jax.shard_map(
        shards,
        mesh=mesh,
        in_specs=(P(None, "lat", "ch", None), P("lat", "ch", None)),
        out_specs=P("lat", "ch", None),
        check_vma=False,
    )
```

profile of v0, /device:TPU:1, one launch (start us, length us, event | category | flops | bytes accessed | tf_op | source)
XLA Modules:
  0.0 162.0 jit_solution(14036317072984009875)
XLA Ops:
  6.5 0.0 copy-start
  6.5 0.0 all-gather.2.cloned.1.call-start
  6.5 19.1 %multiply_convert_fusion = (bf16[1440,704]{1,0:T(8,128)(2,1)S(1)}, bf16[1440,704]{1,0:T(8,128)(2,1)S(1)}) fusion(), kind=kLoop, calls=%fused_computation.3 | loop fusion | flops 14192640 | bytes 4055040 | tf_op jit(solution)/shard_map/convert.1
  25.7 0.0 copy-done
  25.7 1.0 fusion.7
  26.7 0.3 reshape.50
  27.0 1.8 %copy.24 = bf16[2,22,2,2,704]{1,3,2,0,4:T(2,128)(2,1)S(1)} copy(bf16[2,22,2,2,704]{4,3,1,2,0:T(2,128)(2,1)S(1)} %reshape.50) | data formatting | bytes 495616 | tf_op jit(solution)/shard_map/reshape | solution.py:49
  28.8 1.8 %reshape.51 = bf16[32,2,1936]{2,1,0:T(2,128)(2,1)S(1)} reshape(bf16[704,2,2,2,22]{4,3,2,1,0:T(2,128)(2,1)S(1)} %bitcast.45) | data formatting | bytes 495616
  30.6 38.8 %all_to_all.18 = bf16[32,2,1936]{2,1,0:T(2,128)(2,1)S(1)} all-to-all(bf16[32,2,1936]{2,1,0:T(2,128)(2,1)S(1)} %reshape.51), channel_id=1, replica_groups=mesh['lat'=32,'ch'=16] {'lat'}, dimensions={0} | all-to-all | bytes 495616 | tf_op jit(solution)/shard_map/all_to_all | solution.py:50
  69.5 1.8 %reshape.52 = bf16[704,2,2,2,22]{4,3,2,1,0:T(2,128)(2,1)S(1)} reshape(bf16[32,2,1936]{2,1,0:T(2,128)(2,1)S(1)} %all_to_all.18) | data formatting | bytes 495616
  71.3 0.4 copy.50
  71.7 0.0 copy-start.1
  71.7 2.9 %all_to_all.16 = bf16[2,704,2,2,22]{1,3,4,2,0:T(2,128)(2,1)S(1)} reshape(bf16[2,32,22,2,2,22]{2,1,4,5,3,0:T(8,128)(2,1)S(1)} %bitcast.44) | data formatting | bytes 495616 | tf_op jit(solution)/shard_map/all_to_all | solution.py:50
  74.6 0.0 copy-start.2
  74.6 0.2 slice.25
  74.9 0.8 reverse
  75.7 0.3 fusion.19
  76.0 0.1 fusion.20
  76.1 0.4 pad_maximum_fusion.1
  76.5 0.9 copy.27
  77.4 0.0 all-gather.2.cloned.1.call-update
  77.5 0.0 copy-done.1
  77.5 1.0 slice.18
  78.5 0.0 copy-done.2
  78.5 1.0 slice.19
  79.6 56.5 %all-gather.2.cloned.1.call-done = bf16[2,704,32,2,22]{1,3,4,0,2:T(2,128)(2,1)} async-done(((bf16[2,704,2,2,22]{1,3,4,0,2:T(2,128)(2,1)}), bf16[2,704,32,2,22]{1,3,4,0,2:T(2,128)(2,1)}) %all-gather.2.cloned.1.call-update) | async-done | bytes 3964944 | tf_op jit(solution)/shard_map/all_gather | solution.py:59
  136.1 6.5 %fusion.24 = (bf16[2,352,32,2,22]{1,3,4,0,2:T(2,128)(2,1)S(1)}, bf16[2,352,32,2,22]{1,3,4,0,2:T(2,128)(2,1)S(1)}) fusion(bf16[2,704,32,2,22]{1,3,4,0,2:T(2,128)(2,1)} %all-gather.2.cloned.1.call-done), kind=kLoop, calls=%fused_computation.39 | loop fusion | bytes 7929856 | tf_op jit(solution)/shard_map/slice | solution.py:31
  142.6 2.0 %fusion.8 = f32[22,22,2,32,2]{3,1,4,2,0:T(8,128)S(1)} fusion(bf16[2,352,32,2,22]{1,3,4,0,2:T(2,128)(2,1)S(1)} %get-tuple-element.8, bf16[22,22,352]{2,1,0:T(8,128)(2,1)S(1)} %slice.19, bf16[22,22,352]{2,1,0:T(8,128)(2,1)S(1)} %slice.18, pred[22]{0:T(512)(128)(4,1)S(1)} %fusion.21), kind=kOutput, calls=%fused_computation.14 | convolution fusion | flops 43784576 | bytes 2911766 | tf_op jit(solution)/shard_map/mlk,bkcrm->mlbcr/dot_general | solution.py:33
  144.6 2.0 %select_bitcast_fusion.1 = (f32[22,22,1,2,32,2]{4,1,5,3,0,2:T(8,128)S(1)}, f32[22,22,1,2,32,2]{4,1,5,3,0,2:T(8,128)S(1)}) fusion(f32[22,22,2,32,2]{3,1,4,2,0:T(8,128)S(1)} %fusion.8, pred[22]{0:T(512)(128)(4,1)S(1)} %fusion.21, bf16[2,352,32,2,22]{1,3,4,0,2:T(2,128)(2,1)S(1)} %get-tuple-element.7, bf16[22,22,352]{2,1,0:T(8,128)(2,1)S(1)} %slice.18, ...), kind=kOutput, calls=%fused_computation.20 | convolution fusion | flops 43908480 | bytes 3407382 | tf_op jit(solution)/shard_map/mlk,bkcrm->mlbcr/dot_general | solution.py:30
  146.6 1.6 pad_maximum_fusion
  148.2 5.0 %copy.30 = f32[22,22,2,2,32,2]{0,5,4,3,2,1:T(2,128)S(1)} copy(f32[22,22,2,2,32,2]{4,1,5,3,0,2:T(8,128)} %pad_maximum_fusion) | data formatting | bytes 991232 | tf_op jit(solution)/shard_map/stack | solution.py:39
  153.3 1.9 %copy.31 = f32[22,44,128]{2,1,0:T(8,128)} copy(f32[22,44,128]{0,2,1:T(8,128)S(1)} %bitcast.42) | data formatting | bytes 991232 | tf_op jit(solution)/shard_map/reshape;reshape | solution.py:61
  (1 shorter events, 0.0 us)
Async XLA Ops:
  6.5 19.1 %copy-start = (bf16[2,22,2,1440]{3,2,1,0:T(2,128)(2,1)S(1)}, bf16[2,22,2,1440]{3,2,1,0:T(2,128)(2,1)}, u32[]{:S(2)}) copy-start(bf16[2,22,2,1440]{3,2,1,0:T(2,128)(2,1)} %param.2) | copy-start | bytes 760324
  6.5 129.5 %all-gather.2.cloned.1.call-start = ((), (), s32[]{:S(2)}) async-start(), calls=%async_computation.1 | async-start | bytes 4595712 | tf_op jit(solution)/shard_map/all_gather | solution.py:59
  71.7 5.8 %copy-start.1 = (bf16[22,44,352]{2,1,0:T(8,128)(2,1)S(1)}, bf16[22,44,352]{2,1,0:T(8,128)(2,1)}, u32[]{:S(2)}) copy-start(bf16[22,44,352]{2,1,0:T(8,128)(2,1)} %param.3) | copy-start | bytes 2044420
  74.6 3.9 %copy-start.2 = (bf16[22,44,352]{2,1,0:T(8,128)(2,1)S(1)}, bf16[22,44,352]{2,1,0:T(8,128)(2,1)}, u32[]{:S(2)}) copy-start(bf16[22,44,352]{2,1,0:T(8,128)(2,1)} %param.3) | copy-start | bytes 2044420
Sparse Core Ops, SparseCore 0:
  77.6 58.4 all-gather.1
where the time goes:
time: 162 us
  waiting for transfers between devices  56.5 us (35%)
  blocking collectives  38.8 us (24%)
  local copies, waits for them, and re-layouts  26.6 us (16%)
  other arithmetic  21.5 us (13%)
  between operations  13.6 us (8%)
  matrix products  5.07 us (3%)
    all_gather x1, waiting for transfers between devices, shards(): lax.all_gather(parts, 'ch', axis=2, tiled=True)  56.5 us
    all_to_all x1, blocking collectives, shards(): lax.all_to_all(spectrum, 'lat', split_axis=4, concat_axis=1, tiled=True)  38.8 us
    another operation x1, other arithmetic  19.1 us
    slice x1, local copies, waits for them, and re-layouts, parity_project(): parts[:, :hemisphere]  6.52 us
    another operation x1, local copies, waits for them, and re-layouts, parity_project(): joined = jnp.stack([first_out, second_out], axis=2)  5.04 us
    unnamed x9, local copies, waits for them, and re-layouts  4.41 us
    all_to_all x2, local copies, waits for them, and re-layouts, shards(): lax.all_to_all(spectrum, 'lat', split_axis=4, concat_axis=1, tiled=True)  3.34 us
  transfers between devices with their start and end apart: 1, of which 1 were waited for; matrix products, arithmetic and copies ran while one was open for 1% of the time, Pallas kernels for 0%

commit v1 on v0

v1 whole, which is shorter than its diff:
```python
import functools
import math

import numpy as np
import jax
import jax.numpy as jnp
from jax import lax
from jax.experimental import pallas as pl
from jax.experimental.pallas import tpu as pltpu
from jax.sharding import PartitionSpec as P

NLON = 1440
FOLD = NLON // 2
NZ = 16
NLATDEV = 32
SLAB = 22
LBLK = 44
HALF = 352
GROUPS = 3
LP = 48
KP = 384
FP = 768
MESH = pl.DeviceIdType.MESH
NT = (((1,), (1,)), ((), ()))


def slots(g):
    return min(4, SLAB // 2 - 4 * g)


def order_of(g, par, j):
    return 2 * (4 * g + j) + par


def fourier_rows():
    table = np.zeros((GROUPS, 2, NLATDEV, 4, 2, FP), np.float64)
    cols = np.arange(FOLD, dtype=np.int64)
    scale = 1.0 / math.sqrt(NLON)
    owners = np.arange(NLATDEV, dtype=np.int64)[:, None]
    for g in range(GROUPS):
        for par in range(2):
            for j in range(slots(g)):
                order = owners * SLAB + order_of(g, par, j)
                angle = (order * cols[None, :] % NLON) * (2.0 * math.pi / NLON)
                table[g, par, :, j, 0, :FOLD] = np.cos(angle) * scale
                table[g, par, :, j, 1, :FOLD] = -np.sin(angle) * scale
    return table.reshape(GROUPS, 2, NLATDEV * 8, FP).astype(jnp.bfloat16)


def kernel(
    x_ref, f_ref, t_ref, out_ref,
    fv, tv, sb, rb, tg, yf, yp, wb, ob, orr, pm,
    in_sem, z_send, z_recv, t_send, t_recv, p_send, p_recv, o_send, o_recv,
):
    f32, bf16 = jnp.float32, jnp.bfloat16
    lat = lax.axis_index("lat")
    ch = lax.axis_index("ch")
    z, core = lat // 2, lat % 2
    y, x = ch // 4, ch % 4

    f_copy = pltpu.make_async_copy(f_ref, fv, in_sem.at[0])
    t_copy = pltpu.make_async_copy(t_ref, tv, in_sem.at[1])
    f_copy.start()
    t_copy.start()

    def peer(t):
        u, h = t // 2, t % 2
        dz = jnp.where(u % 2 == 1, 8 - (u + 1) // 2, 8 + u // 2)
        return ((z + dz) % NZ) * 2 + (core + 1 + h) % 2

    pq = ((x, y), (y, x))

    def ch_at(par, p, q):
        return q * 4 + p if par == 0 else p * 4 + q

    barrier = pltpu.get_barrier_semaphore()

    def greet(t, carry):
        pl.semaphore_signal(barrier, inc=1, device_id={"lat": peer(t)}, device_id_type=MESH)
        return carry

    lax.fori_loop(0, NLATDEV - 1, greet, 0)
    for d in range(1, 4):
        for par in range(2):
            p, q = pq[par]
            pl.semaphore_signal(
                barrier, inc=1, device_id={"ch": ch_at(par, (p + d) % 4, q)}, device_id_type=MESH
            )

    dst = lax.broadcasted_iota(jnp.int32, (128, 96), 0)
    src = lax.broadcasted_iota(jnp.int32, (128, 96), 1)
    one = jnp.ones_like(dst)
    zero = jnp.zeros_like(dst)
    bc = (
        jnp.where(dst >= SLAB, one, zero)
        + jnp.where(dst >= 2 * SLAB, one, zero)
        + jnp.where(dst >= 3 * SLAB, one, zero)
    )
    k = dst - SLAB * bc
    south = jnp.where(lat >= NLATDEV // 2, 1, 0)
    k = k + south * (SLAB - 1 - 2 * k)
    want = (bc // 2) * (2 * SLAB) + 2 * k + bc % 2
    hit = jnp.logical_and(want == src, dst < 4 * SLAB)
    perm = jnp.where(hit, 1.0, 0.0).astype(bf16)
    xp = [
        jnp.dot(perm, x_ref[par], preferred_element_type=f32).astype(bf16) for par in range(2)
    ]

    f_copy.wait()
    for g in range(GROUPS):
        halves = [
            lax.dot_general(fv[g, par], xp[par], NT, preferred_element_type=f32).reshape(
                NLATDEV, 8, 128
            )
            for par in range(2)
        ]
        sb[g] = jnp.concatenate(halves, axis=1).astype(bf16)
        rb[g, lat] = sb[g, lat]

    t_copy.wait()
    for g in range(GROUPS):
        for par in range(2):
            c = 2 * g + par
            q = pq[par][1]
            tg[c, q] = jnp.zeros((4, LP, KP), bf16)
            if slots(g) < 4:
                for i in range(4):
                    tg[c, i, 3] = jnp.zeros((LP, KP), bf16)
            for j in range(slots(g)):
                tg[c, q, j, :LBLK, :HALF] = tv[order_of(g, par, j)]

    pl.semaphore_wait(barrier, NLATDEV - 1 + 6)

    def z_copy(g, t):
        dest = peer(t)
        return pltpu.make_async_remote_copy(
            src_ref=sb.at[g, dest],
            dst_ref=rb.at[g, lat],
            send_sem=z_send.at[g, dest],
            recv_sem=z_recv.at[g, lat],
            device_id={"lat": dest},
            device_id_type=MESH,
        )

    def z_arrival(g, t):
        source = peer(t)
        return pltpu.make_async_remote_copy(
            src_ref=sb.at[g, source],
            dst_ref=rb.at[g, source],
            send_sem=z_send.at[g, source],
            recv_sem=z_recv.at[g, source],
            device_id={"lat": source},
            device_id_type=MESH,
        )

    for g in range(GROUPS):

        def send(t, carry, g=g):
            z_copy(g, t).start()
            return carry

        lax.fori_loop(0, NLATDEV - 1, send, 0)

    def t_move(c, d):
        g, par = c // 2, c % 2
        p, q = pq[par]
        to, n = (q + d) % 4, slots(g)
        return pltpu.make_async_remote_copy(
            src_ref=tg.at[c, q, pl.ds(0, n)],
            dst_ref=tg.at[c, q, pl.ds(0, n)],
            send_sem=t_send.at[c, d],
            recv_sem=t_recv.at[c, d],
            device_id={"ch": ch_at(par, p, to)},
            device_id_type=MESH,
        )

    def t_arrival(c, d):
        g, par = c // 2, c % 2
        p, q = pq[par]
        frm, n = (q + 4 - d) % 4, slots(g)
        return pltpu.make_async_remote_copy(
            src_ref=tg.at[c, frm, pl.ds(0, n)],
            dst_ref=tg.at[c, frm, pl.ds(0, n)],
            send_sem=t_send.at[c, d],
            recv_sem=t_recv.at[c, d],
            device_id={"ch": ch_at(par, p, frm)},
            device_id_type=MESH,
        )

    def p_move(c, d):
        p, q = pq[c % 2]
        return pltpu.make_async_remote_copy(
            src_ref=yp.at[c],
            dst_ref=wb.at[c, :, p],
            send_sem=p_send.at[c, d],
            recv_sem=p_recv.at[c, d],
            device_id={"ch": ch_at(c % 2, (p + d) % 4, q)},
            device_id_type=MESH,
        )

    def p_arrival(c, d):
        p, q = pq[c % 2]
        frm = (p + 4 - d) % 4
        return pltpu.make_async_remote_copy(
            src_ref=yp.at[c],
            dst_ref=wb.at[c, :, frm],
            send_sem=p_send.at[c, d],
            recv_sem=p_recv.at[c, d],
            device_id={"ch": ch_at(c % 2, frm, q)},
            device_id_type=MESH,
        )

    def o_move(c, d):
        p, q = pq[c % 2]
        to = (q + d) % 4
        return pltpu.make_async_remote_copy(
            src_ref=ob.at[c, to],
            dst_ref=orr.at[c, q],
            send_sem=o_send.at[c, d],
            recv_sem=o_recv.at[c, d],
            device_id={"ch": ch_at(c % 2, p, to)},
            device_id_type=MESH,
        )

    def o_arrival(c, d):
        p, q = pq[c % 2]
        frm = (q + 4 - d) % 4
        return pltpu.make_async_remote_copy(
            src_ref=ob.at[c, frm],
            dst_ref=orr.at[c, frm],
            send_sem=o_send.at[c, d],
            recv_sem=o_recv.at[c, d],
            device_id={"ch": ch_at(c % 2, p, frm)},
            device_id_type=MESH,
        )

    for c in range(2 * GROUPS):
        for d in (1, 3, 2):
            t_move(c, d).start()

    for par in range(2):
        row = lax.broadcasted_iota(jnp.int32, (512, 512), 0)
        col = lax.broadcasted_iota(jnp.int32, (512, 512), 1)
        qq, pp = row // 128, (row // 32) % 4
        chan = ch_at(par, pp, qq)
        want = (
            ((row // 2) % 4) * 128
            + ((row // 16) % 2) * 64
            + chan * 4
            + ((row // 8) % 2) * 2
            + row % 2
        )
        pm[par] = jnp.where(want == col, 1.0, 0.0).astype(bf16)

    lane = lax.broadcasted_iota(jnp.int32, (16, 128), 1)

    def unpack(g):
        def arrived(t, carry):
            z_arrival(g, t).wait_recv()
            return carry

        lax.fori_loop(0, NLATDEV - 1, arrived, 0)
        for b in range(4):
            acc = [[jnp.zeros((16, 128), f32) for _ in range(3)] for _ in range(2)]
            for s in range(NLATDEV // 2):
                north = rb[g, s].astype(f32)
                other = rb[g, NLATDEV - 1 - s].astype(f32)
                first = SLAB * s
                shift = (first - SLAB * b) % 128
                for i, val in enumerate((north + other, north - other)):
                    if shift:
                        val = pltpu.roll(val, shift, 1)
                    for t in range(first // 128, (first + SLAB - 1) // 128 + 1):
                        lo, hi = first - 128 * t, first + SLAB - 128 * t
                        inside = jnp.logical_and(lane >= lo, lane < hi)
                        acc[i][t] = jnp.where(inside, val, acc[i][t])
            for par in range(2):
                for i in range(2):
                    for t in range(3):
                        yf[par, i, b, :, 128 * t : 128 * t + 128] = acc[i][t][
                            8 * par : 8 * par + 8
                        ]
        for par in range(2):
            c = 2 * g + par
            block = yf[par].reshape(2, 32, KP).astype(bf16)
            yp[c] = block
            wb[c, :, pq[par][0]] = block
            for d in (1, 3, 2):
                p_move(c, d).start()

    rows = lax.broadcasted_iota(jnp.int32, (LP, 128), 0)
    lanes = lax.broadcasted_iota(jnp.int32, (LP, 128), 1)
    lane_slot = (lanes // 2) % 4

    def project(c):
        g, par = c // 2, c % 2
        q = pq[par][1]
        for d in (1, 3, 2):
            t_arrival(c, d).wait_recv()
        for d in (1, 3, 2):
            p_arrival(c, d).wait_recv()
        got = lax.dot_general(
            tg[c].reshape(16 * LP, KP),
            wb[c].reshape(256, KP),
            NT,
            preferred_element_type=f32,
        )
        same = rows % 2 == par
        for i in range(4):
            total = jnp.zeros((LP, 128), f32)
            for j in range(slots(g)):
                lo = (4 * i + j) * LP
                both = got[lo : lo + LP]
                val = jnp.where(same, both[:, :128], both[:, 128:])
                total = jnp.where(lane_slot == j, val, total)
            ob[c, i] = total.astype(bf16)
        orr[c, q] = ob[c, q]
        for d in (1, 3, 2):
            o_move(c, d).start()

    def finish(c):
        g, par = c // 2, c % 2
        for d in (1, 3, 2):
            o_arrival(c, d).wait_recv()
        full = jnp.concatenate([orr[c, i] for i in range(4)], axis=1)
        res = jnp.dot(full, pm[par], preferred_element_type=f32)
        for j in range(slots(g)):
            out_ref[order_of(g, par, j)] = res[:LBLK, 128 * j : 128 * j + 128]

    for g in range(GROUPS):
        unpack(g)
        for par in range(2):
            project(2 * g + par)
        if g:
            for par in range(2):
                finish(2 * (g - 1) + par)
    for par in range(2):
        finish(2 * (GROUPS - 1) + par)

    for g in range(GROUPS):

        def sent(t, carry, g=g):
            z_copy(g, t).wait_send()
            return carry

        lax.fori_loop(0, NLATDEV - 1, sent, 0)
    for c in range(2 * GROUPS):
        for d in range(1, 4):
            t_move(c, d).wait_send()
            p_move(c, d).wait_send()
            o_move(c, d).wait_send()


def shards(fields, table):
    wide = fields.astype(jnp.float32)
    first, second = wide[..., :FOLD], wide[..., FOLD:]
    folded = jnp.stack([first + second, first - second]).astype(jnp.bfloat16)
    folded = folded.reshape(2, 4 * SLAB, FOLD)
    folded = jnp.pad(folded, ((0, 0), (0, 96 - 4 * SLAB), (0, FP - FOLD)))
    fourier = jnp.asarray(fourier_rows())
    bf16, f32 = jnp.bfloat16, jnp.float32
    dma = pltpu.SemaphoreType.DMA
    chunks = 2 * GROUPS
    return pl.pallas_call(
        kernel,
        out_shape=jax.ShapeDtypeStruct((SLAB, LBLK, 128), f32),
        in_specs=[
            pl.BlockSpec(memory_space=pltpu.VMEM),
            pl.BlockSpec(memory_space=pl.ANY),
            pl.BlockSpec(memory_space=pl.ANY),
        ],
        out_specs=pl.BlockSpec(memory_space=pltpu.VMEM),
        scratch_shapes=[
            pltpu.VMEM((GROUPS, 2, NLATDEV * 8, FP), bf16),
            pltpu.VMEM((SLAB, LBLK, HALF), bf16),
            pltpu.VMEM((GROUPS, NLATDEV, 16, 128), bf16),
            pltpu.VMEM((GROUPS, NLATDEV, 16, 128), bf16),
            pltpu.VMEM((chunks, 4, 4, LP, KP), bf16),
            pltpu.VMEM((2, 2, 4, 8, KP), f32),
            pltpu.VMEM((chunks, 2, 32, KP), bf16),
            pltpu.VMEM((chunks, 2, 4, 32, KP), bf16),
            pltpu.VMEM((chunks, 4, LP, 128), bf16),
            pltpu.VMEM((chunks, 4, LP, 128), bf16),
            pltpu.VMEM((2, 512, 512), bf16),
            dma((2,)),
            dma((GROUPS, NLATDEV)),
            dma((GROUPS, NLATDEV)),
            dma((chunks, 4)),
            dma((chunks, 4)),
            dma((chunks, 4)),
            dma((chunks, 4)),
            dma((chunks, 4)),
            dma((chunks, 4)),
        ],
        compiler_params=pltpu.CompilerParams(
            collective_id=0, has_side_effects=True, vmem_limit_bytes=48 << 20
        ),
    )(folded, fourier, table)


def solution(mesh):
    return jax.shard_map(
        shards,
        mesh=mesh,
        in_specs=(P(None, "lat", "ch", None), P("lat", "ch", None)),
        out_specs=P("lat", "ch", None),
        check_vma=False,
    )
```

time: 162 us -> 70.2 us (0.43)
  Pallas kernels: 0 us -> 65.3 us
  waiting for transfers between devices: 56.5 us -> 0 us
  blocking collectives: 38.8 us -> 0 us
  local copies, waits for them, and re-layouts: 26.6 us -> 2.11 us
  other arithmetic: 21.5 us -> 1.67 us
  between operations: 13.6 us -> 0.05 us
  matrix products: 5.07 us -> 0 us
    pallas_call x0 -> x1, Pallas kernels: none -> 65.3 us  [shards(): pl.pallas_call(kernel, out_shape=jax.ShapeDtypeStruct((SLAB, LBLK, 128),...]
    all_gather x1 -> x0, waiting for transfers between devices: 56.5 us -> none  [shards(): lax.all_gather(parts, 'ch', axis=2, tiled=True)]
    all_to_all x1 -> x0, blocking collectives: 38.8 us -> none  [shards(): lax.all_to_all(spectrum, 'lat', split_axis=4, concat_axis=1, tiled=True)]
    another operation x2, other arithmetic: 20.7 us -> 0.38 us
    slice x4 -> x0, local copies, waits for them, and re-layouts: 8.85 us -> none  [the longest x1 6.52 us: parity_project(): parts[:, :hemisphere]]
    another operation x2, local copies, waits for them, and re-layouts: 6.95 us -> 0.17 us  [shards(): folded = jnp.stack([first + second, first - second]).astype(jnp.bfloat16)]
    dot_general x3 -> x0, matrix products: 5.07 us -> none  [the longest x1 2.02 us: parity_project(): jnp.einsum('mlk,bkcrm->mlbcr', sym_table, parts[:, :hemisphere], preferre...]
    all_to_all x2 -> x0, local copies, waits for them, and re-layouts: 3.34 us -> none  [shards(): lax.all_to_all(spectrum, 'lat', split_axis=4, concat_axis=1, tiled=True)]
  transfers between devices with their start and end apart: 1 -> 0, of which waited for: 1 -> 0; matrix products, arithmetic and copies ran while one was open for 1% -> 0% of each run, Pallas kernels for 0% -> 0%
where the time goes in v1:
time: 70.2 us; the launch traced here: 69.1 us
  Pallas kernels  65.3 us (93%)
  local copies, waits for them, and re-layouts  2.11 us (3%)
  other arithmetic  1.67 us (2%)
    pallas_call x1, Pallas kernels, shards(): pl.pallas_call(kernel, out_shape=jax.ShapeDtypeStruct((SLAB, LBLK, 128),...  65.3 us
    unnamed x5, local copies, waits for them, and re-layouts  1.94 us

profile of v1, /device:TPU:1, one launch (start us, length us, event | category | flops | bytes accessed | tf_op | source)
XLA Modules:
  0.0 69.1 jit_solution(11589087286672009165)
XLA Ops:
  0.0 0.0 copy-start
  0.0 1.3 %convert_element_type.7 = f32[2,22,2,1440]{3,2,1,0:T(2,128)S(1)} convert(bf16[2,22,2,1440]{3,2,1,0:T(2,128)(2,1)} %param.3) | non-fusion elementwise | flops 126720 | bytes 760320 | tf_op jit(solution)/shard_map/convert_element_type | solution.py:355
  1.3 0.3 add_convert_fusion
  1.6 0.1 stack.9
  1.7 0.1 stack.10
  1.9 0.0 copy-done
  1.9 0.0 copy-start.1
  1.9 1.1 %copy-done.1 = bf16[22,44,352]{2,1,0:T(8,128)(2,1)S(1)} copy-done((bf16[22,44,352]{2,1,0:T(8,128)(2,1)S(1)}, bf16[22,44,352]{2,1,0:T(8,128)(2,1)}, u32[]{:S(2)}) %copy-start.1) | copy-done | bytes 681496
  3.0 65.3 %shard_map.37 = f32[22,44,128]{2,1,0:T(8,128)S(1)} custom-call(bf16[2,96,768]{2,1,0:T(8,128)(2,1)S(1)} %fusion.5.x_ref, bf16[3,2,256,768]{3,2,1,0:T(8,128)(2,1)S(1)} %copy-done, bf16[22,44,352]{2,1,0:T(8,128)(2,1)S(1)} %copy-done.1), custom_call_target="tpu_custom_call" | custom-call | tf_op jit(solution)/shard_map/pallas_call | solution.py:364
  68.3 0.8 %copy.5 = f32[22,44,128]{2,1,0:T(8,128)} copy(f32[22,44,128]{2,1,0:T(8,128)S(1)} %shard_map.37) | data formatting | bytes 991232
  (1 shorter events, 0.0 us)
Async XLA Ops:
  0.0 1.9 %copy-start = (bf16[3,2,256,768]{3,2,1,0:T(8,128)(2,1)S(1)}, bf16[3,2,256,768]{3,2,1,0:T(8,128)(2,1)}, u32[]{:S(2)}) copy-start(bf16[3,2,256,768]{3,2,1,0:T(8,128)(2,1)} %constant.5.clone.f_ref) | copy-start | bytes 7077892
  1.9 1.1 %copy-start.1 = (bf16[22,44,352]{2,1,0:T(8,128)(2,1)S(1)}, bf16[22,44,352]{2,1,0:T(8,128)(2,1)}, u32[]{:S(2)}) copy-start(bf16[22,44,352]{2,1,0:T(8,128)(2,1)} %t_ref.1) | copy-start | bytes 2044420

commit v2 on v1

v2 whole, which is shorter than its diff:
```python
import functools
import math

import numpy as np
import jax
import jax.numpy as jnp
from jax import lax
from jax.experimental import pallas as pl
from jax.experimental.pallas import tpu as pltpu
from jax.sharding import PartitionSpec as P

NLON = 1440
FOLD = NLON // 2
NZ = 16
NLATDEV = 32
SLAB = 22
LBLK = 44
HALF = 352
GROUPS = 3
LP = 48
KP = 384
FP = 768
MESH = pl.DeviceIdType.MESH
NT = (((1,), (1,)), ((), ()))


def slots(g):
    return min(4, SLAB // 2 - 4 * g)


def order_of(g, par, j):
    return 2 * (4 * g + j) + par


def fourier_rows():
    table = np.zeros((GROUPS, 2, NLATDEV, 4, 2, FP), np.float64)
    cols = np.arange(FOLD, dtype=np.int64)
    scale = 1.0 / math.sqrt(NLON)
    owners = np.arange(NLATDEV, dtype=np.int64)[:, None]
    for g in range(GROUPS):
        for par in range(2):
            for j in range(slots(g)):
                order = owners * SLAB + order_of(g, par, j)
                angle = (order * cols[None, :] % NLON) * (2.0 * math.pi / NLON)
                table[g, par, :, j, 0, :FOLD] = np.cos(angle) * scale
                table[g, par, :, j, 1, :FOLD] = -np.sin(angle) * scale
    return table.reshape(GROUPS, 2, NLATDEV * 8, FP).astype(jnp.bfloat16)


def kernel(
    x_ref, f_ref, t_ref, out_ref,
    xv, xs, fv, tv, sb, rb, tg, yf, yp, wb, ob, orr, pm,
    in_sem, z_send, z_recv, t_send, t_recv, p_send, p_recv, o_send, o_recv,
):
    f32, bf16 = jnp.float32, jnp.bfloat16
    lat = lax.axis_index("lat")
    ch = lax.axis_index("ch")
    z, core = lat // 2, lax.rem(lat, 2)
    y, x = ch // 4, lax.rem(ch, 4)

    x_copy = pltpu.make_async_copy(x_ref, xv, in_sem.at[0])
    f_copy = pltpu.make_async_copy(f_ref, fv, in_sem.at[1])
    t_copy = pltpu.make_async_copy(t_ref, tv, in_sem.at[2])
    x_copy.start()
    f_copy.start()
    t_copy.start()

    hops = [8 - (u + 1) // 2 if u % 2 else 8 + u // 2 for u in range(NZ)]
    peers = [lax.rem(z + dz, NZ) * 2 + at for dz in hops for at in (1 - core, core)][:-1]

    pq = ((x, y), (y, x))

    def ch_at(par, p, q):
        return q * 4 + p if par == 0 else p * 4 + q

    barrier = pltpu.get_barrier_semaphore()

    for peer in peers:
        pl.semaphore_signal(barrier, inc=1, device_id={"lat": peer}, device_id_type=MESH)
    for d in range(1, 4):
        for par in range(2):
            p, q = pq[par]
            pl.semaphore_signal(
                barrier, inc=1, device_id={"ch": ch_at(par, lax.rem(p + d, 4), q)}, device_id_type=MESH
            )

    dst = lax.broadcasted_iota(jnp.int32, (128, 96), 0)
    src = lax.broadcasted_iota(jnp.int32, (128, 96), 1)
    one = jnp.ones_like(dst)
    zero = jnp.zeros_like(dst)
    bc = (
        jnp.where(dst >= SLAB, one, zero)
        + jnp.where(dst >= 2 * SLAB, one, zero)
        + jnp.where(dst >= 3 * SLAB, one, zero)
    )
    k = dst - SLAB * bc
    south = jnp.where(lat >= NLATDEV // 2, 1, 0)
    k = k + south * (SLAB - 1 - 2 * k)
    want = (bc // 2) * (2 * SLAB) + 2 * k + bc % 2
    hit = jnp.logical_and(want == src, dst < 4 * SLAB)
    perm = jnp.where(hit, 1.0, 0.0).astype(bf16)
    xs[4 * SLAB :, :] = jnp.zeros((8, 2 * FP), f32)
    xs[:, NLON:] = jnp.zeros((96, 2 * FP - NLON), f32)
    x_copy.wait()
    for i in range(2 * SLAB):
        xs[2 * i : 2 * i + 2, :NLON] = xv[i // SLAB, i % SLAB].astype(f32)
    whole = xs[...]
    first = whole[:, :FP]
    second = pltpu.roll(whole, 2 * FP - FOLD, 1)[:, :FP]
    xp = [
        jnp.dot(perm, val.astype(bf16), preferred_element_type=f32).astype(bf16)
        for val in (first + second, first - second)
    ]

    f_copy.wait()

    def transform(g):
        halves = [
            lax.dot_general(fv[g, par], xp[par], NT, preferred_element_type=f32).reshape(
                NLATDEV, 8, 128
            )
            for par in range(2)
        ]
        sb[g] = jnp.stack(halves, axis=1).astype(bf16)
        rb[g, lat] = sb[g, lat]

    def z_copy(g, dest):
        n = 2 * slots(g)
        return pltpu.make_async_remote_copy(
            src_ref=sb.at[g, dest, :, pl.ds(0, n)],
            dst_ref=rb.at[g, lat, :, pl.ds(0, n)],
            send_sem=z_send.at[g],
            recv_sem=z_recv.at[g],
            device_id={"lat": dest},
            device_id_type=MESH,
        )

    def z_all(g):
        n = 2 * slots(g)
        return pltpu.make_async_remote_copy(
            src_ref=sb.at[g, pl.ds(0, NLATDEV - 1), :, pl.ds(0, n)],
            dst_ref=rb.at[g, pl.ds(0, NLATDEV - 1), :, pl.ds(0, n)],
            send_sem=z_send.at[g],
            recv_sem=z_recv.at[g],
            device_id={"lat": peers[0]},
            device_id_type=MESH,
        )

    def ready_table(g):
        for par in range(2):
            c = 2 * g + par
            q = pq[par][1]
            tg[c, q] = jnp.zeros((4, LP, KP), bf16)
            if slots(g) < 4:
                for i in range(4):
                    tg[c, i, 3] = jnp.zeros((LP, KP), bf16)
            for j in range(slots(g)):
                tg[c, q, j, :LBLK, :HALF] = tv[order_of(g, par, j)]

    def t_move(c, d):
        p, q = pq[c % 2]
        to, n = lax.rem(q + d, 4), slots(c // 2)
        return pltpu.make_async_remote_copy(
            src_ref=tg.at[c, q, pl.ds(0, n)],
            dst_ref=tg.at[c, q, pl.ds(0, n)],
            send_sem=t_send.at[c],
            recv_sem=t_recv.at[c],
            device_id={"ch": ch_at(c % 2, p, to)},
            device_id_type=MESH,
        )

    def t_all(c):
        p, q = pq[c % 2]
        part = tg.at[c, pl.ds(0, 3), pl.ds(0, slots(c // 2))]
        return pltpu.make_async_remote_copy(
            src_ref=part,
            dst_ref=part,
            send_sem=t_send.at[c],
            recv_sem=t_recv.at[c],
            device_id={"ch": ch_at(c % 2, p, lax.rem(q + 1, 4))},
            device_id_type=MESH,
        )

    def p_move(c, d):
        p, q = pq[c % 2]
        return pltpu.make_async_remote_copy(
            src_ref=yp.at[c],
            dst_ref=wb.at[c, :, p],
            send_sem=p_send.at[c],
            recv_sem=p_recv.at[c],
            device_id={"ch": ch_at(c % 2, lax.rem(p + d, 4), q)},
            device_id_type=MESH,
        )

    def p_all(c):
        p, q = pq[c % 2]
        part = wb.at[c, :, pl.ds(0, 3)]
        return pltpu.make_async_remote_copy(
            src_ref=part,
            dst_ref=part,
            send_sem=p_send.at[c],
            recv_sem=p_recv.at[c],
            device_id={"ch": ch_at(c % 2, lax.rem(p + 1, 4), q)},
            device_id_type=MESH,
        )

    def o_move(c, d):
        p, q = pq[c % 2]
        to = lax.rem(q + d, 4)
        return pltpu.make_async_remote_copy(
            src_ref=ob.at[c, to],
            dst_ref=orr.at[c, q],
            send_sem=o_send.at[c],
            recv_sem=o_recv.at[c],
            device_id={"ch": ch_at(c % 2, p, to)},
            device_id_type=MESH,
        )

    def o_all(c):
        p, q = pq[c % 2]
        return pltpu.make_async_remote_copy(
            src_ref=ob.at[c, pl.ds(0, 3)],
            dst_ref=orr.at[c, pl.ds(0, 3)],
            send_sem=o_send.at[c],
            recv_sem=o_recv.at[c],
            device_id={"ch": ch_at(c % 2, p, lax.rem(q + 1, 4))},
            device_id_type=MESH,
        )

    def send_table(g):
        for c in (2 * g, 2 * g + 1):
            for d in (1, 3, 2):
                t_move(c, d).start()

    for g in range(GROUPS):
        transform(g)
        if g == 0:
            t_copy.wait()
            ready_table(0)
            pl.semaphore_wait(barrier, NLATDEV - 1 + 6)
        for peer in peers:
            z_copy(g, peer).start()
        if g < GROUPS - 1:
            if g:
                ready_table(g)
            send_table(g)

    ready_table(GROUPS - 1)

    for par in range(2):
        row = lax.broadcasted_iota(jnp.int32, (512, 512), 0)
        col = lax.broadcasted_iota(jnp.int32, (512, 512), 1)
        qq, pp = row // 128, (row // 32) % 4
        chan = ch_at(par, pp, qq)
        want = (
            ((row // 2) % 4) * 128
            + ((row // 16) % 2) * 64
            + chan * 4
            + ((row // 8) % 2) * 2
            + row % 2
        )
        pm[par] = jnp.where(want == col, 1.0, 0.0).astype(bf16)

    lane = lax.broadcasted_iota(jnp.int32, (16, 128), 1)

    def unpack(g):
        z_all(g).wait_recv()
        for b in range(4):
            acc = [[jnp.zeros((16, 128), f32) for _ in range(3)] for _ in range(2)]
            for s in range(NLATDEV // 2):
                north = rb[g, s].astype(f32).reshape(16, 128)
                other = rb[g, NLATDEV - 1 - s].astype(f32).reshape(16, 128)
                first = SLAB * s
                shift = (first - SLAB * b) % 128
                for i, val in enumerate((north + other, north - other)):
                    if shift:
                        val = pltpu.roll(val, shift, 1)
                    for t in range(first // 128, (first + SLAB - 1) // 128 + 1):
                        lo, hi = first - 128 * t, first + SLAB - 128 * t
                        inside = jnp.logical_and(lane >= lo, lane < hi)
                        acc[i][t] = jnp.where(inside, val, acc[i][t])
            for par in range(2):
                for i in range(2):
                    for t in range(3):
                        yf[par, i, b, :, 128 * t : 128 * t + 128] = acc[i][t][
                            8 * par : 8 * par + 8
                        ]
        for par in range(2):
            c = 2 * g + par
            block = yf[par].reshape(2, 32, KP).astype(bf16)
            yp[c] = block
            wb[c, :, pq[par][0]] = block
            for d in (1, 3, 2):
                p_move(c, d).start()

    rows = lax.broadcasted_iota(jnp.int32, (LP, 128), 0)
    lanes = lax.broadcasted_iota(jnp.int32, (LP, 128), 1)
    lane_slot = (lanes // 2) % 4

    def project(c):
        g, par = c // 2, c % 2
        q = pq[par][1]
        t_all(c).wait_recv()
        p_all(c).wait_recv()
        got = lax.dot_general(
            tg[c].reshape(16 * LP, KP),
            wb[c].reshape(256, KP),
            NT,
            preferred_element_type=f32,
        )
        same = rows % 2 == par
        for i in range(4):
            total = jnp.zeros((LP, 128), f32)
            for j in range(slots(g)):
                lo = (4 * i + j) * LP
                both = got[lo : lo + LP]
                val = jnp.where(same, both[:, :128], both[:, 128:])
                total = jnp.where(lane_slot == j, val, total)
            ob[c, i] = total.astype(bf16)
        orr[c, q] = ob[c, q]
        for d in (1, 3, 2):
            o_move(c, d).start()

    def finish(c):
        g, par = c // 2, c % 2
        o_all(c).wait_recv()
        full = jnp.concatenate([orr[c, i] for i in range(4)], axis=1)
        res = jnp.dot(full, pm[par], preferred_element_type=f32)
        for j in range(slots(g)):
            out_ref[order_of(g, par, j)] = res[:LBLK, 128 * j : 128 * j + 128]

    for g in range(GROUPS):
        unpack(g)
        if g == 0:
            send_table(GROUPS - 1)
        for par in range(2):
            project(2 * g + par)
        if g:
            for par in range(2):
                finish(2 * (g - 1) + par)
    for par in range(2):
        finish(2 * (GROUPS - 1) + par)

    for g in range(GROUPS):
        z_all(g).wait_send()
    for c in range(2 * GROUPS):
        t_all(c).wait_send()
        p_all(c).wait_send()
        o_all(c).wait_send()


def shards(fields, table):
    fourier = jnp.asarray(fourier_rows())
    bf16, f32 = jnp.bfloat16, jnp.float32
    dma = pltpu.SemaphoreType.DMA
    chunks = 2 * GROUPS
    return pl.pallas_call(
        kernel,
        out_shape=jax.ShapeDtypeStruct((SLAB, LBLK, 128), f32),
        in_specs=[
            pl.BlockSpec(memory_space=pl.ANY),
            pl.BlockSpec(memory_space=pl.ANY),
            pl.BlockSpec(memory_space=pl.ANY),
        ],
        out_specs=pl.BlockSpec(memory_space=pltpu.VMEM),
        scratch_shapes=[
            pltpu.VMEM((2, SLAB, 2, NLON), bf16),
            pltpu.VMEM((96, 2 * FP), f32),
            pltpu.VMEM((GROUPS, 2, NLATDEV * 8, FP), bf16),
            pltpu.VMEM((SLAB, LBLK, HALF), bf16),
            pltpu.VMEM((GROUPS, NLATDEV, 2, 8, 128), bf16),
            pltpu.VMEM((GROUPS, NLATDEV, 2, 8, 128), bf16),
            pltpu.VMEM((chunks, 4, 4, LP, KP), bf16),
            pltpu.VMEM((2, 2, 4, 8, KP), f32),
            pltpu.VMEM((chunks, 2, 32, KP), bf16),
            pltpu.VMEM((chunks, 2, 4, 32, KP), bf16),
            pltpu.VMEM((chunks, 4, LP, 128), bf16),
            pltpu.VMEM((chunks, 4, LP, 128), bf16),
            pltpu.VMEM((2, 512, 512), bf16),
            dma((3,)),
            dma((GROUPS,)),
            dma((GROUPS,)),
            dma((chunks,)),
            dma((chunks,)),
            dma((chunks,)),
            dma((chunks,)),
            dma((chunks,)),
            dma((chunks,)),
        ],
        compiler_params=pltpu.CompilerParams(
            collective_id=0, has_side_effects=True, vmem_limit_bytes=62 << 20
        ),
    )(fields, fourier, table)


def solution(mesh):
    return jax.shard_map(
        shards,
        mesh=mesh,
        in_specs=(P(None, "lat", "ch", None), P("lat", "ch", None)),
        out_specs=P("lat", "ch", None),
        check_vma=False,
    )
```

time: 70.2 us -> 55.4 us (0.79)
  Pallas kernels: 65.3 us -> 52.6 us
  other arithmetic: 1.67 us -> 0 us
    pallas_call x1, Pallas kernels: 65.3 us -> 52.6 us  [shards(): pl.pallas_call(kernel, out_shape=jax.ShapeDtypeStruct((SLAB, LBLK, 128),...]
    convert_element_type x1 -> x0, other arithmetic: 1.29 us -> none  [shards(): wide = fields.astype(jnp.float32)]
    unnamed x5 -> x1, local copies, waits for them, and re-layouts: 1.94 us -> 1.88 us
where the time goes in v2:
time: 55.4 us; the launch traced here: 54.5 us
  Pallas kernels  52.6 us (95%)
  local copies, waits for them, and re-layouts  1.88 us (3%)
    pallas_call x1, Pallas kernels, shards(): pl.pallas_call(kernel, out_shape=jax.ShapeDtypeStruct((SLAB, LBLK, 128),...  52.6 us
    unnamed x1, local copies, waits for them, and re-layouts  1.88 us

profile of v2, /device:TPU:1, one launch (start us, length us, event | category | flops | bytes accessed | tf_op | source)
XLA Modules:
  0.0 54.5 jit_solution(12174664053259018697)
XLA Ops:
  0.0 52.6 %shard_map.37 = f32[22,44,128]{2,1,0:T(8,128)} custom-call(bf16[2,22,2,1440]{3,2,1,0:T(2,128)(2,1)} %x_ref.1, bf16[3,2,256,768]{3,2,1,0:T(8,128)(2,1)} %constant.2.clone.f_ref, bf16[22,44,352]{2,1,0:T(8,128)(2,1)} %t_ref.1), custom_call_target="tpu_custom_call" | custom-call | tf_op jit(solution)/shard_map/pallas_call | solution.py:357
  52.6 1.9 %copy.5 = f32[22,44,128]{2,1,0:T(8,128)} copy(f32[22,44,128]{2,1,0:T(8,128)} %shard_map.37) | data formatting | bytes 991232

commit v3 on v2

--- a/solution.py
+++ b/solution.py
@@ -50,7 +50,7 @@
 def kernel(
     x_ref, f_ref, t_ref, out_ref,
     xv, xs, fv, tv, sb, rb, tg, yf, yp, wb, ob, orr, pm,
-    in_sem, z_send, z_recv, t_send, t_recv, p_send, p_recv, o_send, o_recv,
+    in_sem, z_send, z_recv, t_send, t_recv, t_last, p_send, p_recv, o_send, o_recv,
 ):
     f32, bf16 = jnp.float32, jnp.bfloat16
     lat = lax.axis_index("lat")
@@ -169,14 +169,27 @@
             device_id_type=MESH,
         )
 
-    def t_all(c):
-        p, q = pq[c % 2]
-        part = tg.at[c, pl.ds(0, 3), pl.ds(0, slots(c // 2))]
+    def t_pass(c, d):
+        p, q = pq[c % 2]
+        origin, to, n = lax.rem(q + 4 - d, 4), lax.rem(q + d, 4), slots(c // 2)
+        half = pl.ds(0, 2) if d == 1 else pl.ds(2, n - 2)
+        return pltpu.make_async_remote_copy(
+            src_ref=tg.at[c, origin, half],
+            dst_ref=tg.at[c, origin, half],
+            send_sem=t_send.at[c],
+            recv_sem=t_last.at[c],
+            device_id={"ch": ch_at(c % 2, p, to)},
+            device_id_type=MESH,
+        )
+
+    def t_all(c, blocks, recv):
+        p, q = pq[c % 2]
+        part = tg.at[c, pl.ds(0, blocks), pl.ds(0, slots(c // 2))]
         return pltpu.make_async_remote_copy(
             src_ref=part,
             dst_ref=part,
             send_sem=t_send.at[c],
-            recv_sem=t_recv.at[c],
+            recv_sem=recv.at[c],
             device_id={"ch": ch_at(c % 2, p, lax.rem(q + 1, 4))},
             device_id_type=MESH,
         )
@@ -229,8 +242,14 @@
 
     def send_table(g):
         for c in (2 * g, 2 * g + 1):
-            for d in (1, 3, 2):
+            for d in (1, 3):
                 t_move(c, d).start()
+
+    def pass_table(g):
+        for c in (2 * g, 2 * g + 1):
+            t_all(c, 2, t_recv).wait_recv()
+            for d in (1, 3):
+                t_pass(c, d).start()
 
     for g in range(GROUPS):
         transform(g)
@@ -300,7 +319,7 @@
     def project(c):
         g, par = c // 2, c % 2
         q = pq[par][1]
-        t_all(c).wait_recv()
+        t_all(c, 1, t_last).wait_recv()
         p_all(c).wait_recv()
         got = lax.dot_general(
             tg[c].reshape(16 * LP, KP),
@@ -329,22 +348,28 @@
         for j in range(slots(g)):
             out_ref[order_of(g, par, j)] = res[:LBLK, 128 * j : 128 * j + 128]
 
-    for g in range(GROUPS):
-        unpack(g)
-        if g == 0:
-            send_table(GROUPS - 1)
+    def both(step, g):
         for par in range(2):
-            project(2 * g + par)
-        if g:
-            for par in range(2):
-                finish(2 * (g - 1) + par)
-    for par in range(2):
-        finish(2 * (GROUPS - 1) + par)
+            step(2 * g + par)
+
+    pass_table(0)
+    pass_table(1)
+    unpack(0)
+    send_table(2)
+    unpack(1)
+    pass_table(2)
+    both(project, 0)
+    unpack(2)
+    both(project, 1)
+    both(finish, 0)
+    both(project, 2)
+    both(finish, 1)
+    both(finish, 2)
 
     for g in range(GROUPS):
         z_all(g).wait_send()
     for c in range(2 * GROUPS):
-        t_all(c).wait_send()
+        t_all(c, 3, t_recv).wait_send()
         p_all(c).wait_send()
         o_all(c).wait_send()
 
@@ -386,6 +411,7 @@
             dma((chunks,)),
             dma((chunks,)),
             dma((chunks,)),
+            dma((chunks,)),
         ],
         compiler_params=pltpu.CompilerParams(
             collective_id=0, has_side_effects=True, vmem_limit_bytes=62 << 20

time: 55.4 us -> 48.9 us (0.88)
  Pallas kernels: 52.6 us -> 46.6 us
    pallas_call x1, Pallas kernels: 52.6 us -> 46.6 us  [shards(): pl.pallas_call(kernel, out_shape=jax.ShapeDtypeStruct((SLAB, LBLK, 128),...]
where the time goes in v3:
time: 48.9 us; the launch traced here: 48.5 us
  Pallas kernels  46.6 us (95%)
  local copies, waits for them, and re-layouts  1.88 us (4%)
    pallas_call x1, Pallas kernels, shards(): pl.pallas_call(kernel, out_shape=jax.ShapeDtypeStruct((SLAB, LBLK, 128),...  46.6 us
    unnamed x1, local copies, waits for them, and re-layouts  1.88 us

profile of v3, /device:TPU:1, one launch (start us, length us, event | category | flops | bytes accessed | tf_op | source)
XLA Modules:
  0.0 48.5 jit_solution(16567338953504519452)
XLA Ops:
  0.0 46.6 %shard_map.37 = f32[22,44,128]{2,1,0:T(8,128)} custom-call(bf16[2,22,2,1440]{3,2,1,0:T(2,128)(2,1)} %x_ref.1, bf16[3,2,256,768]{3,2,1,0:T(8,128)(2,1)} %constant.2.clone.f_ref, bf16[22,44,352]{2,1,0:T(8,128)(2,1)} %t_ref.1), custom_call_target="tpu_custom_call" | custom-call | tf_op jit(solution)/shard_map/pallas_call | solution.py:382
  46.6 1.9 %copy.5 = f32[22,44,128]{2,1,0:T(8,128)} copy(f32[22,44,128]{2,1,0:T(8,128)} %shard_map.37) | data formatting | bytes 991232

commit v4 on v3

--- a/solution.py
+++ b/solution.py
@@ -24,32 +24,37 @@
 NT = (((1,), (1,)), ((), ()))
 
 
-def slots(g):
-    return min(4, SLAB // 2 - 4 * g)
-
-
-def order_of(g, par, j):
-    return 2 * (4 * g + j) + par
+CHUNKS = (
+    {0: 0, 1: 2, 2: 4, 3: 6},
+    {0: 1, 1: 3, 2: 5, 3: 7},
+    {0: 8, 1: 10, 2: 12, 3: 14},
+    {0: 9, 1: 11, 2: 13, 3: 15},
+    {0: 16, 1: 18, 3: 20},
+    {0: 19, 1: 21, 2: 17},
+)
+SENT = CHUNKS[:5] + ({2: 17}, {0: 19, 1: 21})
+
+
+def pieces(c):
+    return ((0, 2), (3, 1)) if c == 4 else ((0, 2), (2, len(CHUNKS[c]) - 2))
 
 
 def fourier_rows():
-    table = np.zeros((GROUPS, 2, NLATDEV, 4, 2, FP), np.float64)
+    table = np.zeros((len(SENT), NLATDEV, 4, 2, FP), np.float64)
     cols = np.arange(FOLD, dtype=np.int64)
     scale = 1.0 / math.sqrt(NLON)
     owners = np.arange(NLATDEV, dtype=np.int64)[:, None]
-    for g in range(GROUPS):
-        for par in range(2):
-            for j in range(slots(g)):
-                order = owners * SLAB + order_of(g, par, j)
-                angle = (order * cols[None, :] % NLON) * (2.0 * math.pi / NLON)
-                table[g, par, :, j, 0, :FOLD] = np.cos(angle) * scale
-                table[g, par, :, j, 1, :FOLD] = -np.sin(angle) * scale
-    return table.reshape(GROUPS, 2, NLATDEV * 8, FP).astype(jnp.bfloat16)
+    for i, held in enumerate(SENT):
+        for j, local in held.items():
+            angle = ((owners * SLAB + local) * cols[None, :] % NLON) * (2.0 * math.pi / NLON)
+            table[i, :, j, 0, :FOLD] = np.cos(angle) * scale
+            table[i, :, j, 1, :FOLD] = -np.sin(angle) * scale
+    return table.reshape(len(SENT), NLATDEV * 8, FP).astype(jnp.bfloat16)
 
 
 def kernel(
     x_ref, f_ref, t_ref, out_ref,
-    xv, xs, fv, tv, sb, rb, tg, yf, yp, wb, ob, orr, pm,
+    xv, xs, fv, tv, extra, sb, rb, rl, tg, yf, yp, wb, ob, orr, pm,
     in_sem, z_send, z_recv, t_send, t_recv, t_last, p_send, p_recv, o_send, o_recv,
 ):
     f32, bf16 = jnp.float32, jnp.bfloat16
@@ -114,21 +119,33 @@
 
     f_copy.wait()
 
+    def rows_of(i, par):
+        return lax.dot_general(fv[i], xp[par], NT, preferred_element_type=f32)
+
+    wide = lax.broadcasted_iota(jnp.int32, (NLATDEV * 8, 128), 1)
+    spare = jnp.logical_and(wide >= 4 * SLAB, wide < 5 * SLAB)
+
     def transform(g):
-        halves = [
-            lax.dot_general(fv[g, par], xp[par], NT, preferred_element_type=f32).reshape(
-                NLATDEV, 8, 128
-            )
-            for par in range(2)
-        ]
-        sb[g] = jnp.stack(halves, axis=1).astype(bf16)
+        if g == 0:
+            extra[...] = rows_of(4, 0) + rows_of(5, 1)
+        if g < 2:
+            halves = []
+            for par in range(2):
+                own = rows_of(2 * g + par, par)
+                moved = pltpu.roll(extra[...], (4 - (2 * g + par)) * SLAB, 1)
+                halves.append(jnp.where(spare, moved, own).reshape(NLATDEV, 8, 128))
+            sb[g] = jnp.stack(halves, axis=1).astype(bf16)
+        else:
+            sb[g, :, 0] = rows_of(6, 1).reshape(NLATDEV, 8, 128).astype(bf16)
         rb[g, lat] = sb[g, lat]
 
+    def z_part(g):
+        return (slice(None), slice(None)) if g < 2 else (0, pl.ds(0, 4))
+
     def z_copy(g, dest):
-        n = 2 * slots(g)
-        return pltpu.make_async_remote_copy(
-            src_ref=sb.at[g, dest, :, pl.ds(0, n)],
-            dst_ref=rb.at[g, lat, :, pl.ds(0, n)],
+        return pltpu.make_async_remote_copy(
+            src_ref=sb.at[(g, dest) + z_part(g)],
+            dst_ref=rb.at[(g, lat) + z_part(g)],
             send_sem=z_send.at[g],
             recv_sem=z_recv.at[g],
             device_id={"lat": dest},
@@ -136,10 +153,10 @@
         )
 
     def z_all(g):
-        n = 2 * slots(g)
-        return pltpu.make_async_remote_copy(
-            src_ref=sb.at[g, pl.ds(0, NLATDEV - 1), :, pl.ds(0, n)],
-            dst_ref=rb.at[g, pl.ds(0, NLATDEV - 1), :, pl.ds(0, n)],
+        every = (g, pl.ds(0, NLATDEV - 1)) + z_part(g)
+        return pltpu.make_async_remote_copy(
+            src_ref=sb.at[every],
+            dst_ref=rb.at[every],
             send_sem=z_send.at[g],
             recv_sem=z_recv.at[g],
             device_id={"lat": peers[0]},
@@ -151,28 +168,29 @@
             c = 2 * g + par
             q = pq[par][1]
             tg[c, q] = jnp.zeros((4, LP, KP), bf16)
-            if slots(g) < 4:
-                for i in range(4):
-                    tg[c, i, 3] = jnp.zeros((LP, KP), bf16)
-            for j in range(slots(g)):
-                tg[c, q, j, :LBLK, :HALF] = tv[order_of(g, par, j)]
-
-    def t_move(c, d):
-        p, q = pq[c % 2]
-        to, n = lax.rem(q + d, 4), slots(c // 2)
-        return pltpu.make_async_remote_copy(
-            src_ref=tg.at[c, q, pl.ds(0, n)],
-            dst_ref=tg.at[c, q, pl.ds(0, n)],
+            for j in range(4):
+                if j in CHUNKS[c]:
+                    tg[c, q, j, :LBLK, :HALF] = tv[CHUNKS[c][j]]
+                else:
+                    for i in range(4):
+                        tg[c, i, j] = jnp.zeros((LP, KP), bf16)
+
+    def t_move(c, d, piece):
+        p, q = pq[c % 2]
+        part = tg.at[c, q, pl.ds(*piece)]
+        return pltpu.make_async_remote_copy(
+            src_ref=part,
+            dst_ref=part,
             send_sem=t_send.at[c],
             recv_sem=t_recv.at[c],
-            device_id={"ch": ch_at(c % 2, p, to)},
+            device_id={"ch": ch_at(c % 2, p, lax.rem(q + d, 4))},
             device_id_type=MESH,
         )
 
     def t_pass(c, d):
         p, q = pq[c % 2]
-        origin, to, n = lax.rem(q + 4 - d, 4), lax.rem(q + d, 4), slots(c // 2)
-        half = pl.ds(0, 2) if d == 1 else pl.ds(2, n - 2)
+        origin, to = lax.rem(q + 4 - d, 4), lax.rem(q + d, 4)
+        half = pl.ds(*pieces(c)[d // 2])
         return pltpu.make_async_remote_copy(
             src_ref=tg.at[c, origin, half],
             dst_ref=tg.at[c, origin, half],
@@ -184,7 +202,7 @@
 
     def t_all(c, blocks, recv):
         p, q = pq[c % 2]
-        part = tg.at[c, pl.ds(0, blocks), pl.ds(0, slots(c // 2))]
+        part = tg.at[c, pl.ds(0, blocks), pl.ds(0, len(CHUNKS[c]))]
         return pltpu.make_async_remote_copy(
             src_ref=part,
             dst_ref=part,
@@ -243,7 +261,8 @@
     def send_table(g):
         for c in (2 * g, 2 * g + 1):
             for d in (1, 3):
-                t_move(c, d).start()
+                for piece in pieces(c):
+                    t_move(c, d, piece).start()
 
     def pass_table(g):
         for c in (2 * g, 2 * g + 1):
@@ -282,13 +301,32 @@
 
     lane = lax.broadcasted_iota(jnp.int32, (16, 128), 1)
 
+    top = lax.broadcasted_iota(jnp.int32, (8, 128), 0) < 4
+
+    def collect(s):
+        joined = jnp.zeros((8, 128), f32)
+        for b in range(4):
+            moved = pltpu.roll(rb[b // 2, s, b % 2].astype(f32), 128 - (4 - b) * SLAB, 1)
+            inside = jnp.logical_and(lane[:8] >= SLAB * b, lane[:8] < SLAB * (b + 1))
+            joined = jnp.where(inside, moved, joined)
+        rl[s, 0] = joined
+
+    def arrived(g, s):
+        return (rl[s] if g == 2 else rb[g, s].astype(f32)).reshape(16, 128)
+
     def unpack(g):
+        if g == 2:
+            for s in range(NLATDEV):
+                collect(s)
         z_all(g).wait_recv()
+        if g == 2:
+            for s in range(NLATDEV):
+                rl[s, 1] = jnp.where(top, rb[g, s, 0].astype(f32), rl[s, 0])
         for b in range(4):
             acc = [[jnp.zeros((16, 128), f32) for _ in range(3)] for _ in range(2)]
             for s in range(NLATDEV // 2):
-                north = rb[g, s].astype(f32).reshape(16, 128)
-                other = rb[g, NLATDEV - 1 - s].astype(f32).reshape(16, 128)
+                north = arrived(g, s)
+                other = arrived(g, NLATDEV - 1 - s)
                 first = SLAB * s
                 shift = (first - SLAB * b) % 128
                 for i, val in enumerate((north + other, north - other)):
@@ -317,7 +355,7 @@
     lane_slot = (lanes // 2) % 4
 
     def project(c):
-        g, par = c // 2, c % 2
+        par = c % 2
         q = pq[par][1]
         t_all(c, 1, t_last).wait_recv()
         p_all(c).wait_recv()
@@ -330,7 +368,7 @@
         same = rows % 2 == par
         for i in range(4):
             total = jnp.zeros((LP, 128), f32)
-            for j in range(slots(g)):
+            for j in CHUNKS[c]:
                 lo = (4 * i + j) * LP
                 both = got[lo : lo + LP]
                 val = jnp.where(same, both[:, :128], both[:, 128:])
@@ -341,12 +379,12 @@
             o_move(c, d).start()
 
     def finish(c):
-        g, par = c // 2, c % 2
+        par = c % 2
         o_all(c).wait_recv()
         full = jnp.concatenate([orr[c, i] for i in range(4)], axis=1)
         res = jnp.dot(full, pm[par], preferred_element_type=f32)
-        for j in range(slots(g)):
-            out_ref[order_of(g, par, j)] = res[:LBLK, 128 * j : 128 * j + 128]
+        for j, local in CHUNKS[c].items():
+            out_ref[local] = res[:LBLK, 128 * j : 128 * j + 128]
 
     def both(step, g):
         for par in range(2):
@@ -357,14 +395,12 @@
     unpack(0)
     send_table(2)
     unpack(1)
+    unpack(2)
     pass_table(2)
-    both(project, 0)
-    unpack(2)
-    both(project, 1)
-    both(finish, 0)
-    both(project, 2)
-    both(finish, 1)
-    both(finish, 2)
+    for g in range(GROUPS):
+        both(project, g)
+    for g in range(GROUPS):
+        both(finish, g)
 
     for g in range(GROUPS):
         z_all(g).wait_send()
@@ -391,10 +427,12 @@
         scratch_shapes=[
             pltpu.VMEM((2, SLAB, 2, NLON), bf16),
             pltpu.VMEM((96, 2 * FP), f32),
-            pltpu.VMEM((GROUPS, 2, NLATDEV * 8, FP), bf16),
+            pltpu.VMEM((len(SENT), NLATDEV * 8, FP), bf16),
             pltpu.VMEM((SLAB, LBLK, HALF), bf16),
+            pltpu.VMEM((NLATDEV * 8, 128), f32),
             pltpu.VMEM((GROUPS, NLATDEV, 2, 8, 128), bf16),
             pltpu.VMEM((GROUPS, NLATDEV, 2, 8, 128), bf16),
+            pltpu.VMEM((NLATDEV, 2, 8, 128), f32),
             pltpu.VMEM((chunks, 4, 4, LP, KP), bf16),
             pltpu.VMEM((2, 2, 4, 8, KP), f32),
             pltpu.VMEM((chunks, 2, 32, KP), bf16),

time: 48.9 us -> 48.8 us (level)
  no operation moved by 1% of the time
where the time goes in v4:
time: 48.8 us; the launch traced here: 48.7 us
  Pallas kernels  46.8 us (96%)
  local copies, waits for them, and re-layouts  1.88 us (4%)
    pallas_call x1, Pallas kernels, shards(): pl.pallas_call(kernel, out_shape=jax.ShapeDtypeStruct((SLAB, LBLK, 128),...  46.8 us
    unnamed x1, local copies, waits for them, and re-layouts  1.88 us

profile of v4, /device:TPU:1, one launch (start us, length us, event | category | flops | bytes accessed | tf_op | source)
XLA Modules:
  0.0 48.7 jit_solution(5949704997325607769)
XLA Ops:
  0.0 46.8 %shard_map.37 = f32[22,44,128]{2,1,0:T(8,128)} custom-call(bf16[2,22,2,1440]{3,2,1,0:T(2,128)(2,1)} %x_ref.1, bf16[7,256,768]{2,1,0:T(8,128)(2,1)} %constant.2.clone.f_ref, bf16[22,44,352]{2,1,0:T(8,128)(2,1)} %t_ref.1), custom_call_target="tpu_custom_call" | custom-call | tf_op jit(solution)/shard_map/pallas_call | solution.py:418
  46.8 1.9 %copy.5 = f32[22,44,128]{2,1,0:T(8,128)} copy(f32[22,44,128]{2,1,0:T(8,128)} %shard_map.37) | data formatting | bytes 991232

commit v5 on v4

--- a/solution.py
+++ b/solution.py
@@ -278,12 +278,9 @@
             pl.semaphore_wait(barrier, NLATDEV - 1 + 6)
         for peer in peers:
             z_copy(g, peer).start()
-        if g < GROUPS - 1:
-            if g:
-                ready_table(g)
-            send_table(g)
-
-    ready_table(GROUPS - 1)
+        if g:
+            ready_table(g)
+        send_table(g)
 
     for par in range(2):
         row = lax.broadcasted_iota(jnp.int32, (512, 512), 0)
@@ -393,10 +390,9 @@
     pass_table(0)
     pass_table(1)
     unpack(0)
-    send_table(2)
+    pass_table(2)
     unpack(1)
     unpack(2)
-    pass_table(2)
     for g in range(GROUPS):
         both(project, g)
     for g in range(GROUPS):

time: 48.8 us -> 47.7 us (0.977)
  Pallas kernels: 46.8 us -> 45.7 us
    pallas_call x1, Pallas kernels: 46.8 us -> 45.7 us  [shards(): pl.pallas_call(kernel, out_shape=jax.ShapeDtypeStruct((SLAB, LBLK, 128),...]
where the time goes in v5:
time: 47.7 us; the launch traced here: 47.6 us
  Pallas kernels  45.7 us (96%)
  local copies, waits for them, and re-layouts  1.88 us (4%)
    pallas_call x1, Pallas kernels, shards(): pl.pallas_call(kernel, out_shape=jax.ShapeDtypeStruct((SLAB, LBLK, 128),...  45.7 us
    unnamed x1, local copies, waits for them, and re-layouts  1.88 us

profile of v5, /device:TPU:1, one launch (start us, length us, event | category | flops | bytes accessed | tf_op | source)
XLA Modules:
  0.0 47.6 jit_solution(2913913616702373446)
XLA Ops:
  0.0 45.7 %shard_map.37 = f32[22,44,128]{2,1,0:T(8,128)} custom-call(bf16[2,22,2,1440]{3,2,1,0:T(2,128)(2,1)} %x_ref.1, bf16[7,256,768]{2,1,0:T(8,128)(2,1)} %constant.2.clone.f_ref, bf16[22,44,352]{2,1,0:T(8,128)(2,1)} %t_ref.1), custom_call_target="tpu_custom_call" | custom-call | tf_op jit(solution)/shard_map/pallas_call | solution.py:414
  45.7 1.9 %copy.5 = f32[22,44,128]{2,1,0:T(8,128)} copy(f32[22,44,128]{2,1,0:T(8,128)} %shard_map.37) | data formatting | bytes 991232

commit v6 on v5

--- a/solution.py
+++ b/solution.py
@@ -54,8 +54,8 @@
 
 def kernel(
     x_ref, f_ref, t_ref, out_ref,
-    xv, xs, fv, tv, extra, sb, rb, rl, tg, yf, yp, wb, ob, orr, pm,
-    in_sem, z_send, z_recv, t_send, t_recv, t_last, p_send, p_recv, o_send, o_recv,
+    xv, xs, fv, tv, extra, sb, rb, rl, tg, yf, yp, wb, ob, orr, pm, ov,
+    in_sem, z_send, z_recv, t_send, t_recv, t_last, p_send, p_recv, o_send, o_recv, out_sem,
 ):
     f32, bf16 = jnp.float32, jnp.bfloat16
     lat = lax.axis_index("lat")
@@ -381,7 +381,8 @@
         full = jnp.concatenate([orr[c, i] for i in range(4)], axis=1)
         res = jnp.dot(full, pm[par], preferred_element_type=f32)
         for j, local in CHUNKS[c].items():
-            out_ref[local] = res[:LBLK, 128 * j : 128 * j + 128]
+            ov[local] = res[:LBLK, 128 * j : 128 * j + 128]
+            pltpu.make_async_copy(ov.at[local], out_ref.at[local], out_sem.at[c]).start()
 
     def both(step, g):
         for par in range(2):
@@ -396,14 +397,16 @@
     for g in range(GROUPS):
         both(project, g)
     for g in range(GROUPS):
-        both(finish, g)
-
-    for g in range(GROUPS):
         z_all(g).wait_send()
     for c in range(2 * GROUPS):
         t_all(c, 3, t_recv).wait_send()
+    for g in range(GROUPS):
+        both(finish, g)
+    for c in range(2 * GROUPS):
         p_all(c).wait_send()
         o_all(c).wait_send()
+        whole = pl.ds(0, len(CHUNKS[c]))
+        pltpu.make_async_copy(ov.at[whole], out_ref.at[whole], out_sem.at[c]).wait()
 
 
 def shards(fields, table):
@@ -419,7 +422,7 @@
             pl.BlockSpec(memory_space=pl.ANY),
             pl.BlockSpec(memory_space=pl.ANY),
         ],
-        out_specs=pl.BlockSpec(memory_space=pltpu.VMEM),
+        out_specs=pl.BlockSpec(memory_space=pl.ANY),
         scratch_shapes=[
             pltpu.VMEM((2, SLAB, 2, NLON), bf16),
             pltpu.VMEM((96, 2 * FP), f32),
@@ -436,9 +439,11 @@
             pltpu.VMEM((chunks, 4, LP, 128), bf16),
             pltpu.VMEM((chunks, 4, LP, 128), bf16),
             pltpu.VMEM((2, 512, 512), bf16),
+            pltpu.VMEM((SLAB, LBLK, 128), f32),
             dma((3,)),
             dma((GROUPS,)),
             dma((GROUPS,)),
+            dma((chunks,)),
             dma((chunks,)),
             dma((chunks,)),
             dma((chunks,)),

time: 47.7 us -> 47.6 us (level)
  no operation moved by 1% of the time
where the time goes in v6:
time: 47.6 us; the launch traced here: 47.4 us
  Pallas kernels  45.6 us (96%)
  local copies, waits for them, and re-layouts  1.88 us (4%)
    pallas_call x1, Pallas kernels, shards(): pl.pallas_call(kernel, out_shape=jax.ShapeDtypeStruct((SLAB, LBLK, 128),...  45.6 us
    unnamed x1, local copies, waits for them, and re-layouts  1.88 us

profile of v6, /device:TPU:1, one launch (start us, length us, event | category | flops | bytes accessed | tf_op | source)
XLA Modules:
  0.0 47.4 jit_solution(1238150568370779124)
XLA Ops:
  0.0 45.6 %shard_map.37 = f32[22,44,128]{2,1,0:T(8,128)} custom-call(bf16[2,22,2,1440]{3,2,1,0:T(2,128)(2,1)} %x_ref.1, bf16[7,256,768]{2,1,0:T(8,128)(2,1)} %constant.2.clone.f_ref, bf16[22,44,352]{2,1,0:T(8,128)(2,1)} %t_ref.1), custom_call_target="tpu_custom_call" | custom-call | tf_op jit(solution)/shard_map/pallas_call | solution.py:417
  45.6 1.9 %copy.5 = f32[22,44,128]{2,1,0:T(8,128)} copy(f32[22,44,128]{2,1,0:T(8,128)} %shard_map.37) | data formatting | bytes 991232

commit v7 on v6

--- a/solution.py
+++ b/solution.py
@@ -235,9 +235,8 @@
             device_id_type=MESH,
         )
 
-    def o_move(c, d):
-        p, q = pq[c % 2]
-        to = lax.rem(q + d, 4)
+    def o_move(c, to):
+        p, q = pq[c % 2]
         return pltpu.make_async_remote_copy(
             src_ref=ob.at[c, to],
             dst_ref=orr.at[c, q],
@@ -371,9 +370,12 @@
                 val = jnp.where(same, both[:, :128], both[:, 128:])
                 total = jnp.where(lane_slot == j, val, total)
             ob[c, i] = total.astype(bf16)
+
+            @pl.when(q != i)
+            def _(i=i):
+                o_move(c, i).start()
+
         orr[c, q] = ob[c, q]
-        for d in (1, 3, 2):
-            o_move(c, d).start()
 
     def finish(c):
         par = c % 2

time: 47.6 us -> 47.2 us (level)
  Pallas kernels: 45.6 us -> 45.1 us
where the time goes in v7:
time: 47.2 us; the launch traced here: 47 us
  Pallas kernels  45.1 us (96%)
  local copies, waits for them, and re-layouts  1.88 us (4%)
    pallas_call x1, Pallas kernels, shards(): pl.pallas_call(kernel, out_shape=jax.ShapeDtypeStruct((SLAB, LBLK, 128),...  45.1 us
    unnamed x1, local copies, waits for them, and re-layouts  1.88 us

profile of v7, /device:TPU:1, one launch (start us, length us, event | category | flops | bytes accessed | tf_op | source)
XLA Modules:
  0.0 47.0 jit_solution(15946801483763217204)
XLA Ops:
  0.0 45.1 %shard_map.37 = f32[22,44,128]{2,1,0:T(8,128)} custom-call(bf16[2,22,2,1440]{3,2,1,0:T(2,128)(2,1)} %x_ref.1, bf16[7,256,768]{2,1,0:T(8,128)(2,1)} %constant.2.clone.f_ref, bf16[22,44,352]{2,1,0:T(8,128)(2,1)} %t_ref.1), custom_call_target="tpu_custom_call" | custom-call | tf_op jit(solution)/shard_map/pallas_call | solution.py:419
  45.1 1.9 %copy.5 = f32[22,44,128]{2,1,0:T(8,128)} copy(f32[22,44,128]{2,1,0:T(8,128)} %shard_map.37) | data formatting | bytes 991232
